TPU v7x, 128 devices: a whole 4x4x4 slice. The times are simulated.
128 devices in a mesh: row: 32 (over x, z, core), col: 4 (over y).
Axes of the slice: x: 4, y: 4, z: 4, core: 2. Of those that a mesh axis runs over, the one named last changes fastest.
Arguments:
- front: float32 [3, 32, 24, 4, 128, 128], P(None, 'row', None, 'col'), may hold values from -6 to 6
- child_tiles: float32 [8192, 128, 128], P(('row', 'col')), may hold values from -6 to 6
- tile_dest: int32 [8192, 1], P(('row', 'col')), may hold values from 0 to 127; in each aligned block of 64 rows (0 to 63, 64 to 127, ...) no two rows name the same one
- tile_slot: int32 [8192], P(('row', 'col')), may hold values from 0 to 71
- tile_count: int32 [128], P(('row', 'col')), may hold values from 48 to 64, as said below
- diag_inverses: float32 [2, 256, 256], replicated, as said below
Outputs:
- factored: float32 [3, 32, 24, 4, 128, 128], P(None, 'row', None, 'col')
Inputs may be any that keep to these rules, and one draw needn't show every extreme that they name: Among the 64 slots of one device, no two name the same device in tile_dest, live or not; every device is named by some slot. `tile_count`: some device has all 64 slots live. `diag_inverses`: each matrix is upper triangular with a positive diagonal; it is given as it is and need not match any diagonal block of the front.
All inputs are finite; a program needn't handle non-finite values.
Results may differ from a plain program's by a relative error of at most 0.000068.
Values sent between devices are 32-bit elements; how exact they have to be, the bound alone decides.
A program may use at most 128 MiB of HBM per device.

v0:
```python
import jax
import jax.numpy as jnp
from jax import lax
from jax.sharding import PartitionSpec as P


def panel_part(field, inverse, first, my_col, n_col):
    rows_here, tile = (field.shape[0], field.shape[2])
    total = jnp.zeros((rows_here * tile, 2 * tile), jnp.float32)
    for offset in range(2):
        target = first + offset
        local_b = target // n_col
        owner = target % n_col
        column = field[:, local_b].reshape(rows_here * tile, tile)
        term = jnp.dot(
            column, inverse[offset * tile : (offset + 1) * tile], precision=lax.Precision.HIGHEST
        )
        total = total + jnp.where(my_col == owner, term, jnp.zeros_like(term))
    return total


def panel_rows(field, inverse, first, my_row, my_col, n_row, n_col):
    rows_here, tile = (field.shape[0], field.shape[2])
    total = panel_part(field, inverse, first, my_col, n_col).reshape(rows_here, tile, 2 * tile)
    tile_row = jnp.arange(rows_here, dtype=jnp.int32) * n_row + my_row
    total = jnp.where((tile_row >= first)[:, None, None], total, jnp.zeros_like(total))
    summed = lax.psum(total, "col")
    return summed


def column_side(rows_three, cols_here, my_col, n_col):
    rows_here, tile = (rows_three.shape[0], rows_three.shape[1])
    whole = lax.all_gather(
        rows_three.reshape(rows_here, 1, tile, 2 * tile), "row", axis=1, tiled=True
    )
    ordered = whole.reshape(cols_here, n_col, tile, 2 * tile)
    return lax.dynamic_index_in_dim(ordered, my_col, axis=1, keepdims=False)


def trailing(field, rows_three, cols_three, limit, my_row, my_col, n_row, n_col):
    rows_here, cols_here = (field.shape[0], field.shape[1])
    tile_row = jnp.arange(rows_here, dtype=jnp.int32) * n_row + my_row
    tile_col = jnp.arange(cols_here, dtype=jnp.int32) * n_col + my_col
    keep = (tile_row >= limit)[:, None] & (tile_col >= limit)[None, :]
    update = jnp.einsum("aik,bjk->abij", rows_three, cols_three, precision=lax.Precision.HIGHEST)
    return field - jnp.where(keep[:, :, None, None], update, jnp.zeros_like(update))


def body(front, child_tiles, tile_dest, tile_slot, tile_count, diag_inverses):
    n_row = lax.axis_size("row")
    n_col = lax.axis_size("col")
    my_row = lax.axis_index("row")
    my_col = lax.axis_index("col")
    rows_here, cols_here, tile = (front.shape[0], front.shape[2], front.shape[4])
    slots = child_tiles.shape[0]
    devices = n_row * n_col
    live = jnp.arange(slots, dtype=jnp.int32) < tile_count[0]
    hits = (tile_dest[:, 0][None, :] == jnp.arange(devices, dtype=jnp.int32)[:, None]) & live[
        None, :
    ]
    found = jnp.any(hits, axis=1)
    picked = jnp.sum(hits.astype(jnp.int32) * jnp.arange(slots, dtype=jnp.int32)[None, :], axis=1)
    outgoing = jnp.take(child_tiles, picked, axis=0)
    outgoing = jnp.where(found[:, None, None], outgoing, jnp.zeros_like(outgoing))
    slot_out = jnp.where(found, jnp.take(tile_slot, picked).astype(jnp.float32), jnp.float32(-1.0))
    incoming, slot_in = (
        lax.all_to_all(outgoing, ("row", "col"), split_axis=0, concat_axis=0, tiled=True),
        lax.all_to_all(slot_out, ("row", "col"), split_axis=0, concat_axis=0, tiled=True),
    )
    placing = (
        slot_in[None, :] == jnp.arange(rows_here * cols_here, dtype=jnp.float32)[:, None]
    ).astype(jnp.float32)
    added = jnp.dot(
        placing, incoming.reshape(devices, tile * tile), precision=lax.Precision.HIGHEST
    )
    field = front[:, 0, :, 0] + added.reshape(rows_here, cols_here, tile, tile)
    rows_one = panel_rows(field, diag_inverses[0], 0, my_row, my_col, n_row, n_col)
    cols_one = column_side(rows_one, cols_here, my_col, n_col)
    field = trailing(field, rows_one, cols_one, 2, my_row, my_col, n_row, n_col)
    rows_two = panel_rows(field, diag_inverses[1], 2, my_row, my_col, n_row, n_col)
    cols_two = column_side(rows_two, cols_here, my_col, n_col)
    field = trailing(field, rows_two, cols_two, 4, my_row, my_col, n_row, n_col)
    for panel_index, rows_three in ((0, rows_one), (1, rows_two)):
        for offset in range(2):
            target = 2 * panel_index + offset
            local_b = target // n_col
            owner = target % n_col
            piece = rows_three[:, :, offset * tile : (offset + 1) * tile]
            field = field.at[:, local_b].set(jnp.where(my_col == owner, piece, field[:, local_b]))
    return field[:, None, :, None]


def solution(mesh):
    return jax.shard_map(
        body,
        mesh=mesh,
        in_specs=(
            P(None, "row", None, "col", None, None),
            P(("row", "col"), None, None),
            P(("row", "col"), None),
            P(("row", "col")),
            P(("row", "col")),
            P(),
        ),
        out_specs=P(None, "row", None, "col", None, None),
        check_vma=False,
    )
```

profile of v0, /device:TPU:1, one launch (start us, length us, event | category | flops | bytes accessed | tf_op | source)
XLA Modules:
  0.0 462.4 jit_solution(310653920112481245)
XLA Ops:
  10.8 11.5 %all-to-all-start = ((f32[128,1,1]{2,1,0:T(1,128)}), f32[128,1,1]{2,1,0:T(1,128)S(1)}, u32[]{:S(2)}, u32[]{:S(2)}) async-start(f32[128,1,1]{2,1,0:T(1,128)} %copy.46), calls=%async_computation | async-start | bytes 131072 | tf_op jit(solution)/shard_map/all_to_all | solution.py:68
  22.3 6.5 %gather_fusion.1 = f32[128,128,128]{2,1,0:T(8,128)} fusion(f32[64,128,128]{2,1,0:T(8,128)} %param.15, s32[1024]{0:T(1024)S(1)} %pad_clamp_fusion), kind=kCustom, calls=%fused_computation.1 | custom fusion | bytes 16777728 | tf_op jit(solution)/shard_map/jit(_take)/gather | solution.py:63
  28.8 6.4 %select_select_fusion = f32[128,128,128]{2,1,0:T(8,128)} fusion(f32[128,128,128]{2,1,0:T(8,128)} %gather_fusion.1, pred[128]{0:T(512)(128)(4,1)S(1)} %compare_and_fusion, pred[128]{0:T(512)(128)(4,1)S(1)} %fusion.27), kind=kLoop, calls=%fused_computation.4 | loop fusion | flops 4194304 | bytes 16777472 | tf_op jit(solution)/shard_map/jit(_where)/select_n | solution.py:64
  35.2 10.2 %all-to-all-start.1 = ((f32[128,128,128]{2,1,0:T(8,128)}), f32[128,128,128]{2,1,0:T(8,128)}, u32[]{:S(2)}, u32[]{:S(2)}) async-start(f32[128,128,128]{2,1,0:T(8,128)} %select_select_fusion), calls=%async_computation.1 | async-start | bytes 16777216 | tf_op jit(solution)/shard_map/all_to_all | solution.py:67
  46.7 104.0 %all-to-all-done.1 = f32[128,128,128]{2,1,0:T(8,128)} async-done(((f32[128,128,128]{2,1,0:T(8,128)}), f32[128,128,128]{2,1,0:T(8,128)}, u32[]{:S(2)}, u32[]{:S(2)}) %all-to-all-start.1) | async-done | bytes 8388640 | tf_op jit(solution)/shard_map/all_to_all | solution.py:67
  150.8 9.3 %copy.58 = f32[128,128,128]{0,2,1:T(8,128)} copy(f32[128,128,128]{2,1,0:T(8,128)} %all-to-all-done.1) | data formatting | bytes 16777216 | tf_op jit(solution)/shard_map/reshape | solution.py:74
  160.1 12.3 %bitcast_add_fusion = f32[3,24,128,128]{3,1,2,0:T(8,128)S(1)} fusion(f32[3,1,24,1,128,128]{5,4,3,2,1,0:T(8,128)} %param.14, f32[128,128,128]{0,2,1:T(8,128)} %copy.58, f32[3,24]{1,0:T(4,128)S(1)} %multiply_add_fusion, f32[128]{0:T(128)S(1)} %reduce.8), kind=kOutput, calls=%fused_computation.9 | convolution fusion | flops 1813128192 | bytes 17826592 | tf_op jit(solution)/shard_map/dot_general | solution.py:73
  172.4 2.2 copy-done.3
  176.6 37.1 %all-reduce.3.cloned.1.call-done = f32[3,128,256]{2,1,0:T(8,128)} async-done(((f32[3,128,256]{2,1,0:T(8,128)}), f32[3,128,256]{2,1,0:T(8,128)}) %all-reduce.3.cloned.1.call-update) | async-done | bytes 393232 | tf_op jit(solution)/shard_map/psum | solution.py:27
  214.1 68.0 %all-gather.5.cloned.1.call-done = f32[3,4096,256]{2,1,0:T(8,128)} async-done(((f32[3,128,256]{2,1,0:T(8,128)}), f32[3,4096,256]{2,1,0:T(8,128)}) %all-gather.5.cloned.1.call-update) | async-done | bytes 12582928 | tf_op jit(solution)/shard_map/all_gather | solution.py:33
  282.1 6.4 %fusion.6 = f32[24,128,3,128]{1,3,2,0:T(8,128)S(1)} fusion(f32[24,4,128,256]{3,2,1,0:T(8,128)} %bitcast.106, s32[]{:T(128)S(6)} %select_n.140, f32[3,128,256]{2,1,0:T(8,128)} %all-reduce.3.cloned.1.call-done), kind=kOutput, calls=%fused_computation.12 | convolution fusion | flops 3623878656 | bytes 8257540 | tf_op jit(solution)/shard_map/aik,bjk->abij/dot_general | solution.py:45
  288.6 3.2 fusion.3
  291.8 2.2 copy-done.4
  296.2 39.0 %all-reduce.5.cloned.1.call-done = f32[3,128,256]{2,1,0:T(8,128)} async-done(((f32[3,128,256]{2,1,0:T(8,128)}), f32[3,128,256]{2,1,0:T(8,128)}) %all-reduce.5.cloned.1.call-update) | async-done | bytes 393232 | tf_op jit(solution)/shard_map/psum | solution.py:27
  335.3 68.1 %all-gather.7.cloned.1.call-done = f32[3,4096,256]{2,1,0:T(8,128)} async-done(((f32[3,128,256]{2,1,0:T(8,128)}), f32[3,4096,256]{2,1,0:T(8,128)}) %all-gather.7.cloned.1.call-update) | async-done | bytes 12582928 | tf_op jit(solution)/shard_map/all_gather | solution.py:33
  403.5 8.3 %fusion.4 = f32[24,128,3,128]{3,1,2,0:T(8,128)} fusion(f32[24,4,128,256]{3,2,1,0:T(8,128)} %bitcast.107, s32[]{:T(128)S(6)} %select_n.140, f32[3,128,256]{2,1,0:T(8,128)} %all-reduce.5.cloned.1.call-done), kind=kOutput, calls=%fused_computation.10 | convolution fusion | flops 3623878656 | bytes 8257540 | tf_op jit(solution)/shard_map/aik,bjk->abij/dot_general | solution.py:45
  411.8 6.1 %copy.49 = f32[24,128,3,128]{1,0,3,2:T(8,128)} copy(f32[24,128,3,128]{3,1,2,0:T(8,128)} %fusion.4) | data formatting | bytes 9437184 | tf_op jit(solution)/shard_map/aik,bjk->abij/dot_general | solution.py:45
  417.8 4.4 fusion.2
  422.2 2.1 copy-done.2
  424.5 6.5 %scatter.14 = f32[3,1,24,1,128,128]{5,2,4,0,3,1:T(8,128)} dynamic-update-slice(f32[3,1,24,1,128,128]{5,2,4,0,3,1:T(8,128)} %bitcast.97, f32[3,1,1,1,128,128]{5,2,4,0,3,1:T(1,128)S(1)} %bitcast.111, s32[]{:T(128)} %constant.145.clone.1, s32[]{:T(128)} %constant.145.clone.1, s32[]{:T(128)} %constant.145.clone.1, s32[]{:T(128)} %constant.145.clone.1, s32[]{:T(128)} %constant.145.clone.1, ...) | dynamic-update-slice | bytes 393220 | tf_op jit(solution)/shard_map/scatter | solution.py:89
  431.0 6.5 %scatter.15 = f32[3,1,24,1,128,128]{5,2,4,0,3,1:T(8,128)} dynamic-update-slice(f32[3,1,24,1,128,128]{5,2,4,0,3,1:T(8,128)} %scatter.14, f32[3,1,1,1,128,128]{5,2,4,0,3,1:T(1,128)S(1)} %bitcast.110, s32[]{:T(128)} %constant.145.clone.1, s32[]{:T(128)} %constant.145.clone.1, s32[]{:T(128)} %constant.145.clone.1, s32[]{:T(128)} %constant.145.clone.1, s32[]{:T(128)} %constant.145.clone.1, ...) | dynamic-update-slice | bytes 393220 | tf_op jit(solution)/shard_map/scatter | solution.py:89
  437.5 6.5 %scatter.16 = f32[3,1,24,1,128,128]{5,2,4,0,3,1:T(8,128)} dynamic-update-slice(f32[3,1,24,1,128,128]{5,2,4,0,3,1:T(8,128)} %scatter.15, f32[3,1,1,1,128,128]{5,2,4,0,3,1:T(1,128)S(1)} %bitcast.109, s32[]{:T(128)} %constant.145.clone.1, s32[]{:T(128)} %constant.145.clone.1, s32[]{:T(128)} %constant.145.clone.1, s32[]{:T(128)} %constant.145.clone.1, s32[]{:T(128)} %constant.145.clone.1, ...) | dynamic-update-slice | bytes 393220 | tf_op jit(solution)/shard_map/scatter | solution.py:89
  444.0 6.5 %scatter.19 = f32[3,1,24,1,128,128]{5,2,4,0,3,1:T(8,128)} dynamic-update-slice(f32[3,1,24,1,128,128]{5,2,4,0,3,1:T(8,128)} %scatter.16, f32[3,1,1,1,128,128]{5,2,4,0,3,1:T(1,128)S(1)} %bitcast.108, s32[]{:T(128)} %constant.145.clone.1, s32[]{:T(128)} %constant.145.clone.1, s32[]{:T(128)} %constant.145.clone.1, s32[]{:T(128)} %constant.145.clone.1, s32[]{:T(128)} %constant.145.clone.1, ...) | dynamic-update-slice | bytes 393220 | tf_op jit(solution)/shard_map/scatter | solution.py:89
  450.5 5.3 %copy.54 = f32[3,1,24,1,128,128]{5,4,3,2,1,0:T(8,128)} copy(f32[3,1,24,1,128,128]{5,2,4,0,3,1:T(8,128)} %scatter.19) | data formatting | bytes 9437184 | tf_op jit(solution)/shard_map/scatter | solution.py:89
  (55 shorter events, 9.6 us)
Async XLA Ops:
  6.5 2.2 copy-start
  10.8 24.5 %all-to-all-start = ((f32[128,1,1]{2,1,0:T(1,128)}), f32[128,1,1]{2,1,0:T(1,128)S(1)}, u32[]{:S(2)}, u32[]{:S(2)}) async-start(f32[128,1,1]{2,1,0:T(1,128)} %copy.46), calls=%async_computation | async-start | bytes 131072 | tf_op jit(solution)/shard_map/all_to_all | solution.py:68
  35.2 115.6 %all-to-all-start.1 = ((f32[128,128,128]{2,1,0:T(8,128)}), f32[128,128,128]{2,1,0:T(8,128)}, u32[]{:S(2)}, u32[]{:S(2)}) async-start(f32[128,128,128]{2,1,0:T(8,128)} %select_select_fusion), calls=%async_computation.1 | async-start | bytes 16777216 | tf_op jit(solution)/shard_map/all_to_all | solution.py:67
  45.4 168.2 %all-reduce.3.cloned.1.call-start = ((), (), s32[]{:S(2)}) async-start(), calls=%async_computation.2 | async-start | bytes 786432 | tf_op jit(solution)/shard_map/psum | solution.py:27
  160.1 14.6 %copy-start.7 = (f32[2,256,256]{2,1,0:T(8,128)S(1)}, f32[2,256,256]{2,1,0:T(8,128)}, u32[]{:S(2)}) copy-start(f32[2,256,256]{2,1,0:T(8,128)} %param.19) | copy-start | bytes 1572868
  172.4 2.2 copy-start.3
  176.5 112.0 %slice-start = ((s8[4718592]{0:T(1024)(128)(4,1)}), s8[524288]{0:T(1024)(128)(4,1)S(1)}, s32[]{:S(2)}) async-start(s8[4718592]{0:T(1024)(128)(4,1)} %bitcast.98), calls=%async_computation.6 | async-start | bytes 1048576
  176.5 105.5 %all-gather.5.cloned.1.call-start = ((), (), s32[]{:S(2)}) async-start(), calls=%async_computation.4 | async-start | bytes 12976128 | tf_op jit(solution)/shard_map/all_gather | solution.py:33
  213.7 121.5 %all-reduce.5.cloned.1.call-start = ((), (), s32[]{:S(2)}) async-start(), calls=%async_computation.3 | async-start | bytes 786432 | tf_op jit(solution)/shard_map/psum | solution.py:27
  282.1 6.5 %slice-start.1 = ((s8[4718592]{0:T(1024)(128)(4,1)}), s8[4194304]{0:T(1024)(128)(4,1)S(1)}, s32[]{:S(2)}) async-start(s8[4718592]{0:T(1024)(128)(4,1)} %bitcast.98), calls=%async_computation.7 | async-start | bytes 8388608
  291.8 2.2 copy-start.4
  295.9 107.6 %all-gather.7.cloned.1.call-start = ((), (), s32[]{:S(2)}) async-start(), calls=%async_computation.5 | async-start | bytes 12976128 | tf_op jit(solution)/shard_map/all_gather | solution.py:33
  417.8 6.6 %copy-start.5 = (f32[3,128,256]{2,1,0:T(8,128)S(1)}, f32[3,128,256]{2,1,0:T(8,128)}, u32[]{:S(2)}) copy-start(f32[3,128,256]{2,1,0:T(8,128)} %all-reduce.3.cloned.1.call-done) | copy-start | bytes 1179652
  417.8 6.6 %copy-start.6 = (f32[3,128,256]{2,1,0:T(8,128)S(1)}, f32[3,128,256]{2,1,0:T(8,128)}, u32[]{:S(2)}) copy-start(f32[3,128,256]{2,1,0:T(8,128)} %all-reduce.5.cloned.1.call-done) | copy-start | bytes 1179652
  422.2 2.1 copy-start.2
  444.0 11.8 %copy-start.1 = (s32[64]{0:T(128)S(1)}, s32[64]{0:T(128)}, u32[]{:S(2)}) copy-start(s32[64]{0:T(128)} %param.17) | copy-start | bytes 772
Sparse Core Ops, SparseCore 0:
  176.7 36.9 all-reduce.2
  216.0 66.0 all-gather.4
  296.0 39.1 all-reduce.4
  337.4 66.0 all-gather.6
where the time goes:
time: 463 us; the launch traced here: 462 us
  waiting for transfers between devices  316 us (68%)
  local copies, waits for them, and re-layouts  61.9 us (13%)
  matrix products  28.9 us (6%)
  starting transfers between devices  22.5 us (5%)
  other arithmetic  18.5 us (4%)
  between operations  14.1 us (3%)
    all_gather x2, waiting for transfers between devices, column_side(): lax.all_gather(rows_three.reshape(rows_here, 1, tile, 2 * tile), 'row', a...  136 us
    all_to_all x1, waiting for transfers between devices, body(): lax.all_to_all(outgoing, ('row', 'col'), split_axis=0, concat_axis=0, til...  104 us
    psum x2, waiting for transfers between devices, panel_rows(): summed = lax.psum(total, 'col')  76.1 us
    scatter x5, local copies, waits for them, and re-layouts, body(): field.at[:, local_b]  31.3 us
    dot_general x2, matrix products, trailing(): jnp.einsum('aik,bjk->abij', rows_three, cols_three, precision=lax.Precisi...  14.7 us
    dot_general x1, matrix products, body(): jnp.dot(placing, incoming.reshape(devices, tile * tile), precision=lax.Pr...  12.3 us
    all_to_all x1, starting transfers between devices, body(): lax.all_to_all(slot_out, ('row', 'col'), split_axis=0, concat_axis=0, til...  11.5 us
    all_to_all x1, starting transfers between devices, body(): lax.all_to_all(outgoing, ('row', 'col'), split_axis=0, concat_axis=0, til...  10.2 us
  transfers between devices with their start and end apart: 6, of which 5 were waited for; matrix products, arithmetic and copies ran while one was open for 3% of the time, Pallas kernels for 0%

commit v1 on v0

--- a/solution.py
+++ b/solution.py
@@ -1,7 +1,16 @@
+import functools
 import jax
 import jax.numpy as jnp
 from jax import lax
 from jax.sharding import PartitionSpec as P
+
+
+def search_record_over_axis(xs, chip_axis):
+    part_now = jnp.stack(jax.lax.axis_size(chip_axis) * [xs], axis=0)
+    return jnp.concatenate(jax.lax.all_to_all(part_now, chip_axis, 0, 0), axis=1)
+
+
+lead_squares = functools.partial(search_record_over_axis, chip_axis="row")
 
 
 def panel_part(field, inverse, first, my_col, n_col):
@@ -30,9 +39,7 @@
 
 def column_side(rows_three, cols_here, my_col, n_col):
     rows_here, tile = (rows_three.shape[0], rows_three.shape[1])
-    whole = lax.all_gather(
-        rows_three.reshape(rows_here, 1, tile, 2 * tile), "row", axis=1, tiled=True
-    )
+    whole = lead_squares(rows_three.reshape(rows_here, 1, tile, 2 * tile))
     ordered = whole.reshape(cols_here, n_col, tile, 2 * tile)
     return lax.dynamic_index_in_dim(ordered, my_col, axis=1, keepdims=False)
 

time: 463 us -> 778 us (1.68)
  the two profiles are of different devices: /device:TPU:1 before, /device:TPU:36 now
where the time goes in v1:
time: 778 us; the launch traced here: 777 us
  waiting for transfers between devices  579 us (74%)
  local copies, waits for them, and re-layouts  97.4 us (13%)
  starting transfers between devices  35.9 us (5%)
  matrix products  28.7 us (4%)
  other arithmetic  20.8 us (3%)
  between operations  14.3 us (2%)
    all_to_all x2, waiting for transfers between devices, search_record_over_axis(): jax.lax.all_to_all(part_now, chip_axis, 0, 0)  395 us
    all_to_all x1, waiting for transfers between devices, body(): lax.all_to_all(outgoing, ('row', 'col'), split_axis=0, concat_axis=0, til...  98.6 us
    psum x2, waiting for transfers between devices, panel_rows(): summed = lax.psum(total, 'col')  86.1 us
    scatter x5, local copies, waits for them, and re-layouts, body(): field.at[:, local_b]  31.3 us
    all_to_all x2, local copies, waits for them, and re-layouts, search_record_over_axis(): jax.lax.all_to_all(part_now, chip_axis, 0, 0)  21.3 us
  transfers between devices with their start and end apart: 6, of which 5 were waited for; matrix products, arithmetic and copies ran while one was open for 2% of the time, Pallas kernels for 0%

profile of v1, /device:TPU:36, one launch (start us, length us, event | category | flops | bytes accessed | tf_op | source)
XLA Modules:
  0.0 776.6 jit_solution(9012710962859182783)
XLA Ops:
  10.8 10.2 %all-to-all-start = ((f32[128,1,1]{2,1,0:T(1,128)}), f32[128,1,1]{2,1,0:T(1,128)S(1)}, u32[]{:S(2)}, u32[]{:S(2)}) async-start(f32[128,1,1]{2,1,0:T(1,128)} %copy.50), calls=%async_computation | async-start | bytes 131072 | tf_op jit(solution)/shard_map/all_to_all | solution.py:75
  21.0 6.5 gather_fusion.1
  27.5 6.4 select_select_fusion
  33.9 10.2 %all-to-all-start.1 = ((f32[128,128,128]{2,1,0:T(8,128)}), f32[128,128,128]{2,1,0:T(8,128)}, u32[]{:S(2)}, u32[]{:S(2)}) async-start(f32[128,128,128]{2,1,0:T(8,128)} %select_select_fusion), calls=%async_computation.1 | async-start | bytes 16777216 | tf_op jit(solution)/shard_map/all_to_all | solution.py:74
  45.4 98.6 %all-to-all-done.1 = f32[128,128,128]{2,1,0:T(8,128)} async-done(((f32[128,128,128]{2,1,0:T(8,128)}), f32[128,128,128]{2,1,0:T(8,128)}, u32[]{:S(2)}, u32[]{:S(2)}) %all-to-all-start.1) | async-done | bytes 8388640 | tf_op jit(solution)/shard_map/all_to_all | solution.py:74
  144.0 9.3 %copy.64 = f32[128,128,128]{0,2,1:T(8,128)} copy(f32[128,128,128]{2,1,0:T(8,128)} %all-to-all-done.1) | data formatting | bytes 16777216 | tf_op jit(solution)/shard_map/reshape | solution.py:81
  153.3 12.3 %bitcast_add_fusion = f32[3,24,128,128]{3,1,2,0:T(8,128)S(1)} fusion(f32[3,1,24,1,128,128]{5,4,3,2,1,0:T(8,128)} %param.14, f32[128,128,128]{0,2,1:T(8,128)} %copy.64, f32[3,24]{1,0:T(4,128)S(1)} %multiply_add_fusion, f32[128]{0:T(128)S(1)} %reduce.8), kind=kOutput, calls=%fused_computation.9 | convolution fusion | flops 1813128192 | bytes 17826592 | tf_op jit(solution)/shard_map/dot_general | solution.py:80
  169.8 44.8 %all-reduce.3.cloned.1.call-done = f32[3,128,256]{2,1,0:T(8,128)} async-done(((f32[3,128,256]{2,1,0:T(8,128)}), f32[3,128,256]{2,1,0:T(8,128)}) %all-reduce.3.cloned.1.call-update) | async-done | bytes 393232 | tf_op jit(solution)/shard_map/psum | solution.py:36
  214.6 7.0 stack.6
  221.6 7.5 all-to-all-start.2
  229.5 196.5 %all-to-all-done.2 = f32[32,3,1,128,256]{4,3,1,2,0:T(8,128)} async-done(((f32[32,3,1,128,256]{4,3,1,2,0:T(8,128)}), f32[32,3,1,128,256]{4,3,1,2,0:T(8,128)}, u32[]{:S(2)}, u32[]{:S(2)}) %all-to-all-start.2) | async-done | bytes 12582944 | tf_op jit(solution)/shard_map/all_to_all | solution.py:10
  426.0 10.6 %copy.52 = f32[32,3,1,128,256]{4,3,0,1,2:T(8,128)} copy(f32[32,3,1,128,256]{4,3,1,2,0:T(8,128)} %all-to-all-done.2) | data formatting | bytes 25165824 | tf_op jit(solution)/shard_map/all_to_all | solution.py:10
  436.7 6.3 fusion.6
  452.6 41.3 %all-reduce.5.cloned.1.call-done = f32[3,128,256]{2,1,0:T(8,128)} async-done(((f32[3,128,256]{2,1,0:T(8,128)}), f32[3,128,256]{2,1,0:T(8,128)}) %all-reduce.5.cloned.1.call-update) | async-done | bytes 393232 | tf_op jit(solution)/shard_map/psum | solution.py:36
  493.9 7.1 stack.7
  501.0 7.5 all-to-all-start.3
  508.6 198.3 %all-to-all-done.3 = f32[32,3,1,128,256]{4,3,1,2,0:T(8,128)} async-done(((f32[32,3,1,128,256]{4,3,1,2,0:T(8,128)}), f32[32,3,1,128,256]{4,3,1,2,0:T(8,128)}, u32[]{:S(2)}, u32[]{:S(2)}) %all-to-all-start.3) | async-done | bytes 12582944 | tf_op jit(solution)/shard_map/all_to_all | solution.py:10
  706.9 10.7 %copy.54 = f32[32,3,1,128,256]{4,3,0,1,2:T(8,128)} copy(f32[32,3,1,128,256]{4,3,1,2,0:T(8,128)} %all-to-all-done.3) | data formatting | bytes 25165824 | tf_op jit(solution)/shard_map/all_to_all | solution.py:10
  717.6 8.2 %fusion.4 = f32[24,128,3,128]{3,1,2,0:T(8,128)} fusion(f32[24,4,128,256]{3,2,1,0:T(8,128)} %bitcast.102, s32[]{:T(128)S(6)} %select_n.140, f32[3,128,256]{2,1,0:T(8,128)S(1)} %copy-done.6), kind=kOutput, calls=%fused_computation.10 | convolution fusion | flops 3623878656 | bytes 8257540 | tf_op jit(solution)/shard_map/aik,bjk->abij/dot_general | solution.py:52
  725.8 6.1 copy.55
  738.5 6.5 scatter.14
  745.0 6.5 scatter.15
  751.5 6.5 scatter.16
  758.0 6.5 scatter.19
  (52 shorter events, 30.9 us)
Async XLA Ops:
  6.5 2.2 copy-start
  10.8 23.2 %all-to-all-start = ((f32[128,1,1]{2,1,0:T(1,128)}), f32[128,1,1]{2,1,0:T(1,128)S(1)}, u32[]{:S(2)}, u32[]{:S(2)}) async-start(f32[128,1,1]{2,1,0:T(1,128)} %copy.50), calls=%async_computation | async-start | bytes 131072 | tf_op jit(solution)/shard_map/all_to_all | solution.py:75
  33.9 110.1 %all-to-all-start.1 = ((f32[128,128,128]{2,1,0:T(8,128)}), f32[128,128,128]{2,1,0:T(8,128)}, u32[]{:S(2)}, u32[]{:S(2)}) async-start(f32[128,128,128]{2,1,0:T(8,128)} %select_select_fusion), calls=%async_computation.1 | async-start | bytes 16777216 | tf_op jit(solution)/shard_map/all_to_all | solution.py:74
  44.1 170.5 %all-reduce.3.cloned.1.call-start = ((), (), s32[]{:S(2)}) async-start(), calls=%async_computation.4 | async-start | bytes 786432 | tf_op jit(solution)/shard_map/psum | solution.py:36
  153.3 14.6 %copy-start.7 = (f32[2,256,256]{2,1,0:T(8,128)S(1)}, f32[2,256,256]{2,1,0:T(8,128)}, u32[]{:S(2)}) copy-start(f32[2,256,256]{2,1,0:T(8,128)} %param.19) | copy-start | bytes 1572868
  165.7 2.2 copy-start.3
  221.6 204.4 %all-to-all-start.2 = ((f32[32,3,1,128,256]{4,3,1,2,0:T(8,128)}), f32[32,3,1,128,256]{4,3,1,2,0:T(8,128)}, u32[]{:S(2)}, u32[]{:S(2)}) async-start(f32[32,3,1,128,256]{4,3,1,2,0:T(8,128)} %stack.6), calls=%async_computation.2 | async-start | bytes 25165824 | tf_op jit(solution)/shard_map/all_to_all | solution.py:10
  229.2 264.8 %all-reduce.5.cloned.1.call-start = ((), (), s32[]{:S(2)}) async-start(), calls=%async_computation.5 | async-start | bytes 786432 | tf_op jit(solution)/shard_map/psum | solution.py:36
  229.5 207.1 %copy-start.5 = (f32[3,128,256]{2,1,0:T(8,128)S(1)}, f32[3,128,256]{2,1,0:T(8,128)}, u32[]{:S(2)}) copy-start(f32[3,128,256]{2,1,0:T(8,128)} %all-reduce.3.cloned.1.call-done) | copy-start | bytes 1179652
  448.5 2.2 copy-start.4
  501.0 205.9 %all-to-all-start.3 = ((f32[32,3,1,128,256]{4,3,1,2,0:T(8,128)}), f32[32,3,1,128,256]{4,3,1,2,0:T(8,128)}, u32[]{:S(2)}, u32[]{:S(2)}) async-start(f32[32,3,1,128,256]{4,3,1,2,0:T(8,128)} %stack.7), calls=%async_computation.3 | async-start | bytes 25165824 | tf_op jit(solution)/shard_map/all_to_all | solution.py:10
  508.6 209.0 %copy-start.6 = (f32[3,128,256]{2,1,0:T(8,128)S(1)}, f32[3,128,256]{2,1,0:T(8,128)}, u32[]{:S(2)}) copy-start(f32[3,128,256]{2,1,0:T(8,128)} %all-reduce.5.cloned.1.call-done) | copy-start | bytes 1179652
  736.2 2.1 copy-start.2
  758.0 11.8 %copy-start.1 = (s32[64]{0:T(128)S(1)}, s32[64]{0:T(128)}, u32[]{:S(2)}) copy-start(s32[64]{0:T(128)} %param.17) | copy-start | bytes 772
Sparse Core Ops, SparseCore 0:
  169.9 44.6 all-reduce.2
  452.7 41.1 all-reduce.4
